TPU v7x, 512 devices: a whole 4x4x16 slice. The times are simulated.
512 devices in a mesh: ctx: 64 (over y, z), tp: 8 (over x, core).
Axes of the slice: x: 4, y: 4, z: 16, core: 2. Of those that a mesh axis runs over, the one named last changes fastest.
Arguments:
- gate_out: bfloat16 [32768, 4096], P('ctx', 'tp'), may hold values from -6 to 6
- gate_in: bfloat16 [32768, 4096], P('ctx', 'tp'), may hold values from -6 to 6
- signal: bfloat16 [32768, 4096], P('ctx', 'tp'), may hold values from -6 to 6
- decay_rates: float32 [16, 4096], P(None, 'tp'), may hold values from 9.765625e-07 to 0.1, as said below
- residues: float32 [16, 4096], P(None, 'tp'), may hold values from -0.6 to 0.6
- skip_gain: float32 [4096], P('tp'), may hold values from -4 to 4
- out_proj: bfloat16 [4096, 4096], P('tp'), may hold values from -0.09375 to 0.09375
- doc_lengths: int32 [32], replicated, may hold values from 1 to 20480, 32768 in all
Outputs:
- layer_out: bfloat16 [32768, 4096], P(('ctx', 'tp'))
Inputs may be any that keep to these rules, and one draw needn't show every extreme that they name: `doc_lengths`: 32 documents laid end to end, lengths summing to 32768. `decay_rates`: positive.
All inputs are finite; a program needn't handle non-finite values.
Results may differ from a plain program's by a relative error of at most 0.017.
Values may be sent and summed in bfloat16 or wider, within the bound.
No kernel may reach another device: no remote copies, remote signals or barrier semaphores. Data moves between devices by JAX's collectives and lax.ppermute only.
A program may use at most 64 MiB of HBM per device.

v0:
```python
import jax
import jax.numpy as jnp
from jax import lax
from jax.sharding import PartitionSpec as P

precise = lax.Precision.HIGHEST


def per_device(gate_out, gate_in, signal, decay_rates, residues, skip_gain, out_proj, doc_lengths):
    length = signal.shape[0]
    channels = signal.shape[1]
    block_len = min(32, length)
    num_blocks = length // block_len
    my_shard = lax.axis_index("ctx")
    shard_begin = my_shard * length
    doc_ends = jnp.cumsum(doc_lengths)
    doc_starts = doc_ends - doc_lengths
    positions = shard_begin + jnp.arange(length, dtype=jnp.int32)
    doc_index = jnp.sum((doc_starts[None, :] <= positions[:, None]).astype(jnp.int32), axis=1)
    opening = jnp.any(doc_starts[None, :] == positions[:, None], axis=1)
    head_start = jnp.max(jnp.where(doc_starts <= shard_begin, doc_starts, 0))
    open_shard = ((doc_index == doc_index[0]) & (head_start < shard_begin)).astype(jnp.float32)
    anchor = head_start // length
    feed_in = gate_in.astype(jnp.float32) * signal.astype(jnp.float32)
    lag_steps = jnp.arange(block_len, dtype=jnp.float32)
    lag_decay = jnp.exp(-lag_steps[None, :, None] * decay_rates[:, None, :])
    filter_taps = jnp.einsum("nkc,nc->kc", lag_decay, residues, precision=precise)
    lag_ids = jnp.arange(block_len, dtype=jnp.int32)
    onehot = (lag_ids[:, None, None] - lag_ids[None, :, None] == lag_ids[None, None, :]).astype(
        jnp.float32
    )
    toeplitz = jnp.einsum("tsk,kc->tsc", onehot, filter_taps, precision=precise)
    enter_decay = jnp.exp(-(lag_steps + 1.0)[None, :, None] * decay_rates[:, None, :])
    leave_decay = jnp.exp(-(block_len - 1.0 - lag_steps)[None, :, None] * decay_rates[:, None, :])
    block_decay = jnp.exp(-block_len * decay_rates)

    def advance(carry_state, inputs):
        block_rows, block_docs, block_marks = inputs
        same_doc = (block_docs[:, None] == block_docs[None, :]).astype(jnp.float32)
        within = jnp.einsum(
            "tsc,sc->tc", toeplitz * same_doc[:, :, None], block_rows, precision=precise
        )
        before = (jnp.cumsum(block_marks.astype(jnp.int32)) == 0).astype(jnp.float32)
        incoming = (
            jnp.einsum("ntc,nc->tc", enter_decay, residues * carry_state, precision=precise)
            * before[:, None]
        )
        tail_mask = (block_docs == block_docs[block_len - 1]).astype(jnp.float32)
        passes = 1.0 - jnp.max(block_marks.astype(jnp.float32))
        added_state = jnp.einsum(
            "nsc,s,sc->nc", leave_decay, tail_mask, block_rows, precision=precise
        )
        return (block_decay * carry_state * passes + added_state, within + incoming)

    zero_state = jnp.zeros((decay_rates.shape[0], channels), jnp.float32)
    end_state, local_out = lax.scan(
        advance,
        zero_state,
        (
            feed_in.reshape(num_blocks, block_len, channels),
            doc_index.reshape(num_blocks, block_len),
            opening.reshape(num_blocks, block_len),
        ),
    )
    local_out = local_out.reshape(length, channels)
    states_part = lax.all_gather(end_state[None], "ctx", axis=0, tiled=True)
    row_count = states_part.shape[0]
    shard_ids = jnp.arange(row_count, dtype=jnp.int32)
    shard_gap = jnp.maximum(my_shard - 1 - shard_ids, 0).astype(jnp.float32)
    in_window = ((shard_ids >= anchor) & (shard_ids < my_shard)).astype(jnp.float32)
    weight = (
        jnp.exp(-(length * shard_gap)[:, None, None] * decay_rates[None, :, :])
        * in_window[:, None, None]
    )
    carried = jnp.sum(weight * states_part, axis=0)
    offsets = jnp.arange(1, length + 1, dtype=jnp.float32)
    decay_out = jnp.exp(-offsets[None, :, None] * decay_rates[:, None, :])
    from_prior = (
        jnp.einsum("ntc,nc->tc", decay_out, residues * carried, precision=precise)
        * open_shard[:, None]
    )
    conv_total = local_out + from_prior + skip_gain[None, :] * feed_in
    hidden = (gate_out.astype(jnp.float32) * conv_total).astype(jnp.bfloat16)
    return lax.psum_scatter(
        jnp.dot(hidden, out_proj, preferred_element_type=jnp.float32).astype(jnp.bfloat16),
        "tp",
        scatter_dimension=0,
        tiled=True,
    )


def solution(mesh):
    return jax.shard_map(
        per_device,
        mesh=mesh,
        in_specs=(
            P("ctx", "tp"),
            P("ctx", "tp"),
            P("ctx", "tp"),
            P(None, "tp"),
            P(None, "tp"),
            P("tp"),
            P("tp", None),
            P(),
        ),
        out_specs=P(("ctx", "tp"), None),
        check_vma=False,
    )
```

profile of v0, /device:TPU:8, one launch (start us, length us, event | category | flops | bytes accessed | tf_op | source)
XLA Modules:
  0.0 297.7 jit_solution(3338242892878419437)
XLA Ops:
  6.5 0.7 copy.14
  7.5 1.3 fusion.11
  9.1 0.9 multiply_exponential_fusion
  10.0 1.0 multiply_reduce_fusion.5
  11.0 1.0 fusion.8
  12.3 79.1 %while.15 = (s32[]{:T(128)}, f32[16,512]{1,0:T(8,128)S(1)}, f32[16,32,512]{2,1,0:T(8,128)}, f32[16,512]{1,0:T(8,128)S(1)}, pred[16,32]{1,0:T(8,128)(4,1)S(1)}, /...) while((s32[]{:T(128)}, f32[16,512]{1,0:T(8,128)S(1)}, ...), condition=%wide.region_6.7_spmd.clone.clone.clone, body=%wide.region_3.6_spmd.clone.clone.clone.sunk | while | flops 3198147 | bytes 3157015 | solution.py:56
  16.5 0.7 bitcast_dynamic-update-slice_fusion.2
  21.5 0.7 bitcast_dynamic-update-slice_fusion.2
  22.8 0.7 compare_convert_fusion.4
  26.4 0.7 bitcast_dynamic-update-slice_fusion.2
  27.8 0.7 compare_convert_fusion.4
  31.4 0.7 bitcast_dynamic-update-slice_fusion.2
  36.3 0.7 bitcast_dynamic-update-slice_fusion.2
  41.2 0.7 bitcast_dynamic-update-slice_fusion.2
  46.2 0.7 bitcast_dynamic-update-slice_fusion.2
  51.1 0.7 bitcast_dynamic-update-slice_fusion.2
  57.5 0.7 compare_convert_fusion.4
  61.0 0.7 bitcast_dynamic-update-slice_fusion.2
  62.4 0.7 compare_convert_fusion.4
  66.0 0.7 bitcast_dynamic-update-slice_fusion.2
  67.3 0.7 compare_convert_fusion.4
  70.9 0.7 bitcast_dynamic-update-slice_fusion.2
  77.2 0.7 compare_convert_fusion.4
  80.8 0.7 bitcast_dynamic-update-slice_fusion.2
  85.8 0.7 bitcast_dynamic-update-slice_fusion.2
  90.7 0.7 bitcast_dynamic-update-slice_fusion.2
  96.0 140.3 %all-gather.3.cloned.1.call-done = f32[1024,512]{1,0:T(8,128)} async-done(((f32[16,512]{1,0:T(8,128)}), f32[1024,512]{1,0:T(8,128)}) %all-gather.3.cloned.1.call-update) | async-done | bytes 2097168 | tf_op jit(solution)/shard_map/all_gather | solution.py:66
  236.4 2.1 multiply_reduce_fusion.4
  238.5 2.8 multiply_reduce_fusion.3
  241.8 1.8 copy-done.10
  243.6 4.3 %convolution_convert_fusion = bf16[512,4096]{1,0:T(8,128)(2,1)} fusion(bf16[512,512]{1,0:T(8,128)(2,1)S(1)} %fusion.7, bf16[512,4096]{1,0:T(8,128)(2,1)S(1)} %copy-done.10), kind=kOutput, calls=%fused_computation.19 | convolution fusion | flops 2149580800 | bytes 8912896 | tf_op jit(solution)/shard_map/dot_general | solution.py:85
  248.0 42.9 %reduce-scatter.2.cloned.1.call-done = bf16[64,4096]{1,0:T(8,128)(2,1)} async-done(((bf16[512,4096]{1,0:T(8,128)(2,1)}), bf16[64,4096]{1,0:T(8,128)(2,1)}) %reduce-scatter.2.cloned.1.call-update) | async-done | bytes 524304 | tf_op jit(solution)/shard_map/reduce_scatter | solution.py:84
  (297 shorter events, 56.1 us)
Async XLA Ops:
  6.5 229.8 %all-gather.3.cloned.1.call-start = ((), (), s32[]{:S(2)}) async-start(), calls=%async_computation.2 | async-start | bytes 2129920 | tf_op jit(solution)/shard_map/all_gather | solution.py:66
  9.1 2.9 copy-start
  9.1 3.0 copy-start.2
  11.0 1.2 copy-start.4
  11.0 1.2 copy-start.8
  91.4 0.6 copy-start.5
  92.0 198.8 %reduce-scatter.2.cloned.1.call-start = ((), (), s32[]{:S(2)}) async-start(), calls=%async_computation.1 | async-start | bytes 4718592 | tf_op jit(solution)/shard_map/reduce_scatter | solution.py:84
  238.5 2.9 copy-start.1
  238.5 2.9 copy-start.3
  238.5 2.9 copy-start.6
  238.5 2.9 copy-start.7
  238.5 2.9 copy-start.9
  241.4 2.2 copy-start.10
Sparse Core Ops, SparseCore 0:
  92.2 144.1 all-gather.2
  248.1 42.7 reduce-scatter.1
where the time goes:
time: 298 us
  waiting for transfers between devices  183 us (61%)
  other arithmetic  64.3 us (22%)
  between operations  16.4 us (6%)
  local copies, waits for them, and re-layouts  16.3 us (5%)
  loops' own time  12 us (4%)
  matrix products  5.35 us (2%)
    all_gather x1, waiting for transfers between devices, per_device(): states_part = lax.all_gather(end_state[None], 'ctx', axis=0, tiled=True)  140 us
    reduce_scatter x1, waiting for transfers between devices, per_device(): lax.psum_scatter(jnp.dot(hidden, out_proj, preferred_element_type=jnp.flo...  42.9 us
    another operation x34, other arithmetic  12.2 us
    another operation x1, loops' own time, per_device(): lax.scan(advance, zero_state, (feed_in.reshape(num_blocks, block_len, cha...  12 us
    dynamic_update_slice x16, other arithmetic, per_device(): lax.scan(advance, zero_state, (feed_in.reshape(num_blocks, block_len, cha...  11.2 us
    reduce_max x16, other arithmetic, advance(): passes = 1.0 - jnp.max(block_marks.astype(jnp.float32))  11.1 us
    slice x16, local copies, waits for them, and re-layouts, advance(): tail_mask = (block_docs == block_docs[block_len - 1]).astype(jnp.float32)  10.6 us
    dot_general x16, other arithmetic, advance(): jnp.einsum('tsc,sc->tc', toeplitz * same_doc[:, :, None], block_rows, pre...  7.12 us
  transfers between devices with their start and end apart: 2, of which 2 were waited for; matrix products, arithmetic and copies ran while one was open for 0% of the time, Pallas kernels for 0%

commit v1 on v0

--- a/solution.py
+++ b/solution.py
@@ -2,6 +2,7 @@
 import jax.numpy as jnp
 from jax import lax
 from jax.sharding import PartitionSpec as P
+from jax.lax import all_to_all, axis_size
 
 precise = lax.Precision.HIGHEST
 
@@ -63,7 +64,16 @@
         ),
     )
     local_out = local_out.reshape(length, channels)
-    states_part = lax.all_gather(end_state[None], "ctx", axis=0, tiled=True)
+    lead_signs_on = lambda incoming_x: jnp.concatenate(
+        all_to_all(
+            jnp.stack([incoming_x] * axis_size("ctx"), 0),
+            axis_name="ctx",
+            split_axis=0,
+            concat_axis=0,
+        ),
+        axis=0,
+    )
+    states_part = lead_signs_on(end_state[None])
     row_count = states_part.shape[0]
     shard_ids = jnp.arange(row_count, dtype=jnp.int32)
     shard_gap = jnp.maximum(my_shard - 1 - shard_ids, 0).astype(jnp.float32)

time: 298 us -> 266 us (0.89)
  waiting for transfers between devices: 183 us -> 133 us
  starting transfers between devices: 0.04 us -> 18.8 us
    all_gather x1 -> x0, waiting for transfers between devices: 140 us -> none  [per_device(): states_part = lax.all_gather(end_state[None], 'ctx', axis=0, tiled=True)]
    all_to_all x0 -> x1, waiting for transfers between devices: none -> 93.5 us  [per_device(): all_to_all(jnp.stack([incoming_x] * axis_size('ctx'), 0), axis_name='ctx'...]
    all_to_all x0 -> x1, starting transfers between devices: none -> 18.7 us  [per_device(): all_to_all(jnp.stack([incoming_x] * axis_size('ctx'), 0), axis_name='ctx'...]
    reduce_scatter x1, waiting for transfers between devices: 42.9 us -> 39.5 us  [per_device(): lax.psum_scatter(jnp.dot(hidden, out_proj, preferred_element_type=jnp.flo...]
where the time goes in v1:
time: 266 us
  waiting for transfers between devices  133 us (50%)
  other arithmetic  62.8 us (24%)
  starting transfers between devices  18.8 us (7%)
  local copies, waits for them, and re-layouts  17.3 us (7%)
  between operations  16.4 us (6%)
  loops' own time  12 us (5%)
  matrix products  5.36 us (2%)
    all_to_all x1, waiting for transfers between devices, per_device(): all_to_all(jnp.stack([incoming_x] * axis_size('ctx'), 0), axis_name='ctx'...  93.5 us
    reduce_scatter x1, waiting for transfers between devices, per_device(): lax.psum_scatter(jnp.dot(hidden, out_proj, preferred_element_type=jnp.flo...  39.5 us
    all_to_all x1, starting transfers between devices, per_device(): all_to_all(jnp.stack([incoming_x] * axis_size('ctx'), 0), axis_name='ctx'...  18.7 us
    another operation x34, other arithmetic  12.2 us
    another operation x1, loops' own time, per_device(): lax.scan(advance, zero_state, (feed_in.reshape(num_blocks, block_len, cha...  12 us
    dynamic_update_slice x16, other arithmetic, per_device(): lax.scan(advance, zero_state, (feed_in.reshape(num_blocks, block_len, cha...  11.2 us
    reduce_max x16, other arithmetic, advance(): passes = 1.0 - jnp.max(block_marks.astype(jnp.float32))  11.1 us
    slice x16, local copies, waits for them, and re-layouts, advance(): tail_mask = (block_docs == block_docs[block_len - 1]).astype(jnp.float32)  10.6 us
  transfers between devices with their start and end apart: 2, of which 2 were waited for; matrix products, arithmetic and copies ran while one was open for 0% of the time, Pallas kernels for 0%

profile of v1, /device:TPU:8, one launch (start us, length us, event | category | flops | bytes accessed | tf_op | source)
XLA Modules:
  0.0 265.6 jit_solution(12416678031092720459)
XLA Ops:
  6.5 0.7 copy.16
  7.5 1.3 fusion.12
  9.1 0.9 multiply_exponential_fusion
  10.0 1.0 multiply_reduce_fusion.4
  11.0 1.0 fusion.9
  12.3 79.1 %while.15 = (s32[]{:T(128)}, f32[16,512]{1,0:T(8,128)S(1)}, f32[16,32,512]{2,1,0:T(8,128)}, f32[16,512]{1,0:T(8,128)S(1)}, pred[16,32]{1,0:T(8,128)(4,1)S(1)}, /...) while((s32[]{:T(128)}, f32[16,512]{1,0:T(8,128)S(1)}, ...), condition=%wide.region_6.7_spmd.clone.clone.clone, body=%wide.region_3.6_spmd.clone.clone.clone.sunk | while | flops 3198147 | bytes 3157015 | solution.py:57
  13.0 0.7 compare_convert_fusion.4
  16.5 0.7 bitcast_dynamic-update-slice_fusion.2
  21.5 0.7 bitcast_dynamic-update-slice_fusion.2
  26.4 0.7 bitcast_dynamic-update-slice_fusion.2
  31.4 0.7 bitcast_dynamic-update-slice_fusion.2
  36.3 0.7 bitcast_dynamic-update-slice_fusion.2
  37.7 0.7 compare_convert_fusion.4
  41.2 0.7 bitcast_dynamic-update-slice_fusion.2
  42.6 0.7 compare_convert_fusion.4
  46.2 0.7 bitcast_dynamic-update-slice_fusion.2
  47.6 0.7 compare_convert_fusion.4
  51.1 0.7 bitcast_dynamic-update-slice_fusion.2
  61.0 0.7 bitcast_dynamic-update-slice_fusion.2
  66.0 0.7 bitcast_dynamic-update-slice_fusion.2
  70.9 0.7 bitcast_dynamic-update-slice_fusion.2
  80.8 0.7 bitcast_dynamic-update-slice_fusion.2
  82.2 0.7 compare_convert_fusion.4
  85.8 0.7 bitcast_dynamic-update-slice_fusion.2
  90.7 0.7 bitcast_dynamic-update-slice_fusion.2
  91.4 1.6 stack.3
  93.0 18.7 %all-to-all-start = ((f32[64,1,16,512]{3,2,1,0:T(8,128)}), f32[64,1,16,512]{3,2,1,0:T(8,128)S(1)}, u32[]{:S(2)}, u32[]{:S(2)}) async-start(f32[64,1,16,512]{3,2,1,0:T(8,128)} %stack.3), calls=%async_computation | async-start | bytes 4194304 | tf_op jit(solution)/shard_map/all_to_all | solution.py:68
  115.8 93.5 %all-to-all-done = f32[64,1,16,512]{3,2,1,0:T(8,128)S(1)} async-done(((f32[64,1,16,512]{3,2,1,0:T(8,128)}), f32[64,1,16,512]{3,2,1,0:T(8,128)S(1)}, u32[]{:S(2)}, u32[]{:S(2)}) %all-to-all-start) | async-done | bytes 2097184 | tf_op jit(solution)/shard_map/all_to_all | solution.py:68
  209.8 2.8 %multiply_reduce_fusion.3 = f32[512,512]{0,1:T(8,128)S(1)} fusion(f32[512,16]{0,1:T(8,128)S(1)} %multiply_bitcast_fusion.1, f32[16,512]{1,0:T(8,128)S(1)} %get-tuple-element.333, f32[512]{0:T(512)S(1)} %add_negate_fusion), kind=kLoop, calls=%fused_computation.18 | loop fusion | flops 12320768 | bytes 1116160 | tf_op jit(solution)/shard_map/ntc,nc->tc/dot_general | solution.py:89
  213.1 1.8 copy-done.9
  214.9 4.3 %convolution_convert_fusion = bf16[512,4096]{1,0:T(8,128)(2,1)} fusion(bf16[512,512]{1,0:T(8,128)(2,1)S(1)} %fusion.8, bf16[512,4096]{1,0:T(8,128)(2,1)S(1)} %copy-done.9), kind=kOutput, calls=%fused_computation.19 | convolution fusion | flops 2149580800 | bytes 8912896 | tf_op jit(solution)/shard_map/dot_general | solution.py:95
  219.3 39.5 %reduce-scatter.2.cloned.1.call-done = bf16[64,4096]{1,0:T(8,128)(2,1)} async-done(((bf16[512,4096]{1,0:T(8,128)(2,1)}), bf16[64,4096]{1,0:T(8,128)(2,1)}) %reduce-scatter.2.cloned.1.call-update) | async-done | bytes 524304 | tf_op jit(solution)/shard_map/reduce_scatter | solution.py:94
  (295 shorter events, 56.7 us)
Async XLA Ops:
  9.1 3.0 %copy-start = (bf16[512,512]{1,0:T(8,128)(2,1)S(1)}, bf16[512,512]{1,0:T(8,128)(2,1)}, u32[]{:S(2)}) copy-start(bf16[512,512]{1,0:T(8,128)(2,1)} %param.12) | copy-start | bytes 1572868
  9.1 3.0 %copy-start.2 = (bf16[512,512]{1,0:T(8,128)(2,1)S(1)}, bf16[512,512]{1,0:T(8,128)(2,1)}, u32[]{:S(2)}) copy-start(bf16[512,512]{1,0:T(8,128)(2,1)} %param.11) | copy-start | bytes 1572868
  11.0 1.2 copy-start.4
  11.0 1.2 copy-start.7
  93.0 116.2 %all-to-all-start = ((f32[64,1,16,512]{3,2,1,0:T(8,128)}), f32[64,1,16,512]{3,2,1,0:T(8,128)S(1)}, u32[]{:S(2)}, u32[]{:S(2)}) async-start(f32[64,1,16,512]{3,2,1,0:T(8,128)} %stack.3), calls=%async_computation | async-start | bytes 4194304 | tf_op jit(solution)/shard_map/all_to_all | solution.py:68
  111.8 147.0 %reduce-scatter.2.cloned.1.call-start = ((), (), s32[]{:S(2)}) async-start(), calls=%async_computation.2 | async-start | bytes 4718592 | tf_op jit(solution)/shard_map/reduce_scatter | solution.py:94
  209.8 2.9 %copy-start.1 = (bf16[512,512]{1,0:T(8,128)(2,1)S(1)}, bf16[512,512]{1,0:T(8,128)(2,1)}, u32[]{:S(2)}) copy-start(bf16[512,512]{1,0:T(8,128)(2,1)} %param.12) | copy-start | bytes 1572868
  209.8 2.9 %copy-start.3 = (bf16[512,512]{1,0:T(8,128)(2,1)S(1)}, bf16[512,512]{1,0:T(8,128)(2,1)}, u32[]{:S(2)}) copy-start(bf16[512,512]{1,0:T(8,128)(2,1)} %param.11) | copy-start | bytes 1572868
  209.8 2.9 %copy-start.5 = (f32[16,32,512]{2,1,0:T(8,128)S(1)}, f32[16,32,512]{2,1,0:T(8,128)}, u32[]{:S(2)}) copy-start(f32[16,32,512]{2,1,0:T(8,128)} %get-tuple-element.63) | copy-start | bytes 3145732
  209.8 2.9 %copy-start.6 = (bf16[512,512]{1,0:T(8,128)(2,1)S(1)}, bf16[512,512]{1,0:T(8,128)(2,1)}, u32[]{:S(2)}) copy-start(bf16[512,512]{1,0:T(8,128)(2,1)} %param.10) | copy-start | bytes 1572868
  209.8 2.9 %copy-start.8 = (f32[512]{0:T(512)S(1)}, f32[512]{0:T(512)}, u32[]{:S(2)}) copy-start(f32[512]{0:T(512)} %param.15) | copy-start | bytes 6148
  212.7 2.2 copy-start.9
Sparse Core Ops, SparseCore 0:
  219.4 39.3 reduce-scatter.1
